TPU v7x, 128 devices: a whole 4x4x4 slice. The times are simulated.
128 devices in a mesh: tm: 128 (over z, x, y, core).
Axes of the slice: x: 4, y: 4, z: 4, core: 2. Of those that a mesh axis runs over, the one named last changes fastest.
Arguments:
- measurements: float32 [1024, 192, 512], P('tm'), may hold values from -8 to 8
- observed: int32 [1024], P('tm'), may hold values 0 or 1
- segment_ids: int32 [1024], P('tm'), may hold values from 0 to 31, never falling along the last dimension, each value on 1 to 64 neighbouring positions
- courant_table: float32 [32, 4], replicated, may hold values from 0.15 to 0.6
- filter_gains: float32 [192], replicated, may hold values from 0.0005 to 0.08
- initial_state: float32 [192, 512], replicated, may hold values from -6 to 6
Outputs:
- filtered: float32 [1024, 192, 512], P('tm')
- consistency: float32 [512], replicated
Inputs may be any that keep to these rules, and one draw needn't show every extreme that they name: `segment_ids`: the segment number never falls along time; each segment lasts 1 to 64 steps, one exactly that.
All inputs are finite; a program needn't handle non-finite values. No bound on the sum of `observed` on one device may be relied on, other than what follows from the above.
Results may differ from a plain program's by a relative error of at most 0.0003.
Values sent between devices are 32-bit elements; how exact they have to be, the bound alone decides.
A program may use at most 192 MiB of HBM per device.

v0:
```python
import jax
import jax.numpy as jnp
from jax import lax
from jax.sharding import PartitionSpec as P

CABLES = 4
HALF = 24
SEGS = 32


PAYLOAD = 0.3
HIGHEST = lax.Precision.HIGHEST


def prefix(part, axis, combine, identity):
    place = lax.axis_index(axis)
    gathered = jax.tree.map(lambda a: lax.all_gather(a, axis), part)
    state = jax.tree.map(lambda a, e: jnp.zeros_like(a) + jnp.asarray(e, a.dtype), part, identity)

    def one(turn, state):
        return combine(
            state, jax.tree.map(lambda a: lax.dynamic_index_in_dim(a, turn, 0, False), gathered)
        )

    return lax.fori_loop(0, place, one, state)


def coupling_pattern():
    count = CABLES * HALF
    indices = jnp.arange(count)
    cable_of = indices // HALF
    node_of = indices % HALF
    same = cable_of[:, None] == cable_of[None, :]
    lower = same & (indices[:, None] == indices[None, :] + 1)
    ends = (node_of[:, None] == HALF - 1) & (node_of[None, :] == HALF - 1) & jnp.logical_not(same)
    pattern = (
        jnp.eye(count, dtype=jnp.float32)
        - lower.astype(jnp.float32)
        - PAYLOAD * ends.astype(jnp.float32)
    )
    return (pattern, cable_of)


def transitions_from(courant):
    pattern, cable_of = coupling_pattern()
    member = (cable_of[:, None] == jnp.arange(CABLES)[None, :]).astype(jnp.float32)
    row_scale = jnp.einsum("sc,rc->sr", courant, member, precision=HIGHEST)
    coupled = row_scale[:, :, None] * pattern[None]
    gram = jnp.einsum("sji,sjk->sik", coupled, coupled, precision=HIGHEST)
    ident = jnp.broadcast_to(jnp.eye(pattern.shape[0], dtype=jnp.float32), coupled.shape)
    upper_rows = jnp.concatenate([ident - gram, -jnp.swapaxes(coupled, 1, 2)], axis=2)
    lower_rows = jnp.concatenate([coupled, ident], axis=2)
    return jnp.concatenate([upper_rows, lower_rows], axis=1)


def matmul(left, right):
    return jnp.dot(left, right, precision=HIGHEST, preferred_element_type=jnp.float32)


def compose(earlier, later):
    return (matmul(later[0], earlier[0]), matmul(later[0], earlier[1]) + later[1])


def local(measurements, observed, segment_ids, courant_table, filter_gains, initial_state):
    steps_here = measurements.shape[0]
    states = measurements.shape[1]
    flights = measurements.shape[2]
    selector = (segment_ids[:, None] == jnp.arange(SEGS)[None, :]).astype(jnp.float32)
    courant = jnp.dot(
        selector, courant_table, precision=HIGHEST, preferred_element_type=jnp.float32
    )
    transitions = transitions_from(courant)
    weights = observed.astype(jnp.float32)
    keep_factor = 1.0 - weights[:, None] * filter_gains[None, :]
    affine_maps = keep_factor[:, :, None] * transitions
    affine_shifts = weights[:, None, None] * filter_gains[None, :, None] * measurements
    identity_map = jnp.eye(states, dtype=jnp.float32)
    zero_shift = jnp.zeros((states, flights), jnp.float32)

    def fold_local(carry, element):
        return (compose(carry, element), None)

    (block_map, block_shift), unused = lax.scan(
        fold_local, (identity_map, zero_shift), (affine_maps, affine_shifts)
    )
    prefix_map, prefix_shift = prefix(
        (block_map, block_shift), "tm", compose, (identity_map, zero_shift)
    )
    start_state = matmul(prefix_map, initial_state) + prefix_shift

    def advance(state, inputs):
        transition, weight, sample = inputs
        predicted = matmul(transition, state)
        innovation = sample - predicted
        updated = predicted + weight * filter_gains[:, None] * innovation
        power = weight * jnp.sum(innovation * innovation, axis=0)
        return (updated, (updated, power))

    unused_state, (filtered, powers) = lax.scan(
        advance, start_state, (transitions, weights, measurements)
    )
    partial_power = jnp.sum(powers, axis=0)
    total_power = lax.psum(partial_power, "tm")
    consistency = total_power / (steps_here * lax.axis_size("tm") * states)
    return (filtered, consistency)


def solution(mesh):
    in_specs = (P("tm", None, None), P("tm"), P("tm"), P(), P(), P())
    out_specs = (P("tm", None, None), P())
    return jax.shard_map(local, mesh=mesh, in_specs=in_specs, out_specs=out_specs, check_vma=False)
```

profile of v0, /device:TPU:0, one launch (start us, length us, event | category | flops | bytes accessed | tf_op | source)
XLA Modules:
  0.0 762.6 jit_solution(17322322415439356978)
XLA Ops:
  8.7 1.7 convolution_subtract_fusion
  11.8 3.9 broadcast_multiply_fusion.2
  15.8 1.7 maximum_maximum_fusion
  17.4 18.6 %while.41 = (s32[]{:T(128)}, f32[192,192]{1,0:T(8,128)S(1)}, f32[192,512]{1,0:T(8,128)S(1)}, f32[8,192,192]{1,2,0:T(8,128)S(1)}, f32[8,192,512]{2,1,0:T(8,128)}, /*index=5*/s32[]{:T(128)}, s32[]{:T(128)}) while((s32[]{:T(128)}, f32[192,192]{1,0:T(8,128)S(1)}, f32[192,512]{1,0:T(8,128)S(1)}, f32[8,192,192]{1,2,0:T(8,128)S(1)}, ...), condition=%wide.region_1.2_spmd.clone, body=%wide.region_0.1_spmd.clone.sunk | while | flops 311623680 | bytes 2999387 | solution.py:83
  17.4 1.7 convolution_add_fusion.6
  19.8 1.7 convolution_add_fusion.6
  22.1 1.7 convolution_add_fusion.6
  24.4 1.7 convolution_add_fusion.6
  26.8 1.7 convolution_add_fusion.6
  29.1 1.7 convolution_add_fusion.6
  31.4 1.7 convolution_add_fusion.6
  33.8 1.7 convolution_add_fusion.6
  37.5 94.9 %all-gather.5.cloned.1.call-done = f32[24576,192]{1,0:T(8,128)} async-done(((f32[192,192]{1,0:T(8,128)}), f32[24576,192]{1,0:T(8,128)}) %all-gather.5.cloned.1.call-update) | async-done | bytes 18874384 | tf_op jit(solution)/shard_map/all_gather | solution.py:17
  132.5 137.3 %all-gather.7.cloned.1.call-done = f32[24576,512]{1,0:T(8,128)} async-done(((f32[192,512]{1,0:T(8,128)}), f32[24576,512]{1,0:T(8,128)}) %all-gather.7.cloned.1.call-update) | async-done | bytes 50331664 | tf_op jit(solution)/shard_map/all_gather | solution.py:17
  270.5 45.3 %while.40 = (s32[]{:T(128)}, f32[192,512]{1,0:T(8,128)S(1)}, f32[8,192,512]{2,1,0:T(8,128)}, f32[8,512]{1,0:T(8,128)S(1)}, f32[8,192,192]{1,2,0:T(8,128)}, /*ind...) while((s32[]{:T(128)}, f32[192,512]{1,0:T(8,128)S(1)}, ...), condition=%wide.region_6.7_spmd, body=%wide.region_4.6_spmd.sunk | while | flops 227082432 | bytes 3749249 | solution.py:99
  271.8 2.5 bitcast_dynamic-update-slice_fusion.2
  277.5 2.5 bitcast_dynamic-update-slice_fusion.2
  283.2 2.5 bitcast_dynamic-update-slice_fusion.2
  288.8 2.5 bitcast_dynamic-update-slice_fusion.2
  294.5 2.5 bitcast_dynamic-update-slice_fusion.2
  300.2 2.5 bitcast_dynamic-update-slice_fusion.2
  305.8 2.5 bitcast_dynamic-update-slice_fusion.2
  311.5 2.5 bitcast_dynamic-update-slice_fusion.2
  315.9 439.3 %psum.7 = f32[512]{0:T(512)S(1)} all-reduce(f32[512]{0:T(512)S(1)} %reduce_sum.18), channel_id=1, replica_groups=mesh['tm'=128] {'tm'}, use_global_device_ids=true, to_apply=%region_8.9 | all-reduce | flops 512 | bytes 4096 | tf_op jit(solution)/shard_map/psum | solution.py:103
  (106 shorter events, 35.3 us)
Async XLA Ops:
  7.2 262.7 %copy-start = (f32[192,512]{1,0:T(8,128)S(1)}, f32[192,512]{1,0:T(8,128)}, u32[]{:S(2)}) copy-start(f32[192,512]{1,0:T(8,128)} %param.17) | copy-start | bytes 1179652
  7.2 125.3 %all-gather.5.cloned.1.call-start = ((), (), s32[]{:S(2)}) async-start(), calls=%async_computation | async-start | bytes 25362432 | tf_op jit(solution)/shard_map/all_gather | solution.py:17
  11.8 3.9 copy-start.3
  36.1 0.7 copy-start.2
  36.1 0.8 copy-start.1
  36.8 233.0 %all-gather.7.cloned.1.call-start = ((), (), s32[]{:S(2)}) async-start(), calls=%async_computation.1 | async-start | bytes 50724864 | tf_op jit(solution)/shard_map/all_gather | solution.py:17
  269.8 0.7 copy-start.4
Sparse Core Ops, SparseCore 0:
  36.9 95.5 all-gather.4
  135.6 134.1 all-gather.6
where the time goes:
time: 770 us; the launch traced here: 763 us
  blocking collectives  439 us (57%)
  waiting for transfers between devices  233 us (30%)
  matrix products  41.7 us (5%)
  other arithmetic  26.6 us (3%)
  between operations  14.2 us (2%)
    psum x1, blocking collectives, local(): total_power = lax.psum(partial_power, 'tm')  439 us
    all_gather x2, waiting for transfers between devices, prefix(): gathered = jax.tree.map(lambda a: lax.all_gather(a, axis), part)  232 us
    dot_general x25, matrix products, matmul(): jnp.dot(left, right, precision=HIGHEST, preferred_element_type=jnp.float32)  39 us
  transfers between devices with their start and end apart: 2, of which 2 were waited for; matrix products, arithmetic and copies ran while one was open for 0% of the time, Pallas kernels for 0%

commit v1 on v0

v1 whole, which is shorter than its diff:
```python
import functools

import jax
import jax.numpy as jnp
from jax import lax
from jax.experimental import pallas as pl
from jax.experimental.pallas import tpu as pltpu
from jax.sharding import PartitionSpec as P

CABLES = 4
HALF = 24
SIDE = CABLES * HALF
STATES = 2 * SIDE
SEGS = 32
PAYLOAD = 0.3
CORES = 2
MESH = pl.DeviceIdType.MESH
VREGS = SIDE // 8
F32 = jnp.float32


def torus_of(devices):
    return {128: (4, 4, 4), 16: (2, 2, 2)}[devices]


def lanes(tile):
    return pl.ds(pl.multiple_of(tile * 128, 128), 128)


class Rows:
    def __init__(self):
        row = lax.broadcasted_iota(jnp.int32, (8, 128), 0)
        self.first = row == 0
        self.last = row == 7
        self.pay = jnp.where(self.last, F32(PAYLOAD), F32(0.0))
        self.zero = jnp.zeros((8, 128), F32)
        self.low = lax.broadcasted_iota(jnp.int32, (8, 128), 1) < 64


def leap(rows, q, p, w):
    rolled = [pltpu.roll(v, 1, 0) for v in q]
    total = (q[2] + q[5]) + (q[8] + q[11])
    new_p, u = [], []
    for v in range(VREGS):
        before = jnp.where(rows.first, rolled[v - 1] if v % 3 else rows.zero, rolled[v])
        d = q[v] - before
        if v % 3 == 2:
            d = d - rows.pay * (total - q[v])
        new_p.append(p[v] + w[v // 3] * d)
        u.append(w[v // 3] * new_p[v])
    rolled = [pltpu.roll(v, 7, 0) for v in u]
    total = (u[2] + u[5]) + (u[8] + u[11])
    new_q = []
    for v in range(VREGS):
        after = jnp.where(rows.last, rolled[v + 1] if v % 3 < 2 else rows.zero, rolled[v])
        e = u[v] - after
        if v % 3 == 2:
            e = e - rows.pay * (total - u[v])
        new_q.append(q[v] - e)
    return new_q, new_p


def pack(rows, q, p, half):
    if half == 0:
        return [jnp.where(rows.low, a, pltpu.roll(b, 64, 1)) for a, b in zip(q, p)]
    return [jnp.where(rows.low, pltpu.roll(a, 64, 1), b) for a, b in zip(q, p)]


def kernel(
    dims, runs, steps,
    seg_ref, obs_ref, table_ref, gains_ref, m_hbm, x0_hbm,
    out_hbm, power_ref,
    mb, x0b, gain_rows, keep, params_v, params_s, bpack, bin_, maps, prefix, xin, sums, zin, zout,
    start, sout, sin, powers,
    m_sem, out_sem, loc_sem,
    par_s, par_r, up_s, up_r, mx_s, mx_r, mp_s, mp_r, x_s, x_r, z_s, z_r, dn_s, dn_r, pw_s, pw_r,
):
    nz, nx, ny = dims
    ring = ny * CORES
    here = steps
    tiles = runs // 128
    me = lax.axis_index("tm")
    r = lax.rem(me, ring)
    core = lax.rem(me, CORES)
    x = lax.rem(me // ring, nx)
    z = me // (ring * nx)
    base = me - r
    rows = Rows()

    def ring_dev(k):
        return base + lax.rem(r + k, ring)

    def x_dev(k):
        return (z * nx + lax.rem(x + k, nx)) * ring + r

    def z_dev(k):
        return (lax.rem(z + k, nz) * nx + x) * ring + r

    def send(src, dst, ssem, rsem, dev):
        return pltpu.make_async_remote_copy(
            src_ref=src, dst_ref=dst, send_sem=ssem, recv_sem=rsem, device_id=(dev,), device_id_type=MESH
        )

    loads = []
    for f in range(tiles):
        c = pltpu.make_async_copy(m_hbm.at[:, :, pl.ds(f * 128, 128)], mb.at[f], m_sem.at[f])
        c.start()
        loads.append(c)

    barrier = pltpu.get_barrier_semaphore()
    for k in range(1, ring):
        pl.semaphore_signal(barrier, inc=1, device_id=(ring_dev(k),), device_id_type=MESH)
    for k in range(1, nx):
        pl.semaphore_signal(barrier, inc=1, device_id=(x_dev(k),), device_id_type=MESH)
    for k in range(1, nz):
        pl.semaphore_signal(barrier, inc=1, device_id=(z_dev(k),), device_id_type=MESH)

    @pl.when(me == 0)
    def _():
        c = pltpu.make_async_copy(x0_hbm, x0b, loc_sem.at[0])
        c.start()
        c.wait()

    @pl.when(me > 0)
    def _():
        x0b[...] = jnp.zeros_like(x0b)

    row_i = lax.broadcasted_iota(jnp.int32, (8, 128), 0)
    lane_i = lax.broadcasted_iota(jnp.int32, (8, 128), 1)
    tile = jnp.zeros((8, 128), jnp.int32)
    for t in range(here):
        tile = jnp.where((row_i == 0) & (lane_i == t), seg_ref[t], tile)
        tile = jnp.where((row_i == 1) & (lane_i == t), obs_ref[t], tile)
    params_v[r] = tile

    for v in range(STATES // 8):
        spread = jnp.zeros((8, 1), F32)
        for part in range(2):
            g = jnp.broadcast_to(gains_ref[0:1, part * 128 : part * 128 + 128], (8, 128))
            spread = spread + jnp.sum(
                jnp.where(lane_i + part * 128 == row_i + v * 8, g, F32(0.0)), axis=1, keepdims=True
            )
        g = jnp.broadcast_to(spread, (8, 128))
        gain_rows[pl.ds(v * 8, 8), :] = g
        keep[0, pl.ds(v * 8, 8), :] = jnp.ones((8, 128), F32)
        keep[1, pl.ds(v * 8, 8), :] = 1.0 - g

    pl.semaphore_wait(barrier, (ring - 1) + (nx - 1) + (nz - 1))

    par = []
    for k in range(1, ring):
        c = send(params_v.at[r], params_v.at[r], par_s.at[k], par_r.at[k], ring_dev(k))
        c.start()
        par.append(c)

    def load_state(ref_q):
        return (
            [ref_q[pl.ds(v * 8, 8), :] for v in range(VREGS)],
            [ref_q[pl.ds(SIDE + v * 8, 8), :] for v in range(VREGS)],
        )

    def own_w(t):
        s = seg_ref[t]
        return [table_ref[s, c] for c in range(CABLES)]

    ups = {}
    for f in range(tiles):
        loads[f].wait()

        def one(t, carry, f=f):
            q, p = list(carry[:VREGS]), list(carry[VREGS:])
            q, p = leap(rows, q, p, own_w(t))
            o = obs_ref[t].astype(F32)
            new = []
            for v, pred in enumerate(q + p):
                inn = mb[f, t, pl.ds(v * 8, 8), :] - pred
                new.append(pred + (o * gain_rows[pl.ds(v * 8, 8), :]) * inn)
            return tuple(new)

        q, p = load_state(x0b.at[:, pl.ds(f * 128, 128)])
        state = lax.fori_loop(0, here, one, tuple(q + p))
        q, p = list(state[:VREGS]), list(state[VREGS:])
        for half in range(2):
            packed = pack(rows, q, p, half)
            for v in range(VREGS):
                bpack[2 * f + half, pl.ds(v * 8, 8), :] = packed[v]
    for k in range(1, ring):
        peer = lax.rem(r + k, ring)
        c = send(bpack.at[peer], bin_.at[r], up_s.at[k], up_r.at[k], ring_dev(k))
        c.start()
        ups[k] = c
    own = pltpu.make_async_copy(bpack.at[r], bin_.at[r], loc_sem.at[1])
    own.start()

    for c in par:
        c.wait()
    ints = pltpu.make_async_copy(params_v, params_s, loc_sem.at[2])
    ints.start()
    ints.wait()

    def step_free(carry, j, t):
        q, p = list(carry[:VREGS]), list(carry[VREGS:])
        s = params_s[j, 0, t]
        o = params_s[j, 1, t]
        q, p = leap(rows, q, p, [table_ref[s, c] for c in range(CABLES)])
        return tuple(a * keep[o, pl.ds(v * 8, 8), :] for v, a in enumerate(q + p))

    def block_free(carry, j):
        return lax.fori_loop(0, here, lambda t, s: step_free(s, j, t), carry)

    col = lane_i + core * 128
    state = tuple(jnp.where(col == row_i + v * 8, F32(1.0), F32(0.0)) for v in range(2 * VREGS))
    state = lax.fori_loop(0, ring, lambda j, s: block_free(s, j), state)
    for v in range(2 * VREGS):
        maps[x, pl.ds(v * 8, 8), lanes(core)] = state[v]
    mine = maps.at[x, :, lanes(core)]
    mate = me + 1 - 2 * core
    mxs = []
    for k in range(1, nx):
        c = send(mine, mine, mx_s.at[k], mx_r.at[k], x_dev(k))
        c.start()
        mxs.append(c)
    mps = [send(mine, mine, mp_s.at[0], mp_r.at[0], mate)]
    mps[0].start()

    for k in range(1, ring):
        ups[k].wait()
    own.wait()

    def unpack(ref):
        a = [ref[pl.ds(v * 8, 8), :] for v in range(VREGS)]
        return a, [pltpu.roll(v, 64, 1) for v in a]

    q, p = unpack(bin_.at[0])

    def rise(j, carry):
        carry = block_free(carry, j)
        q, p = unpack(bin_.at[j])
        return tuple(a + b for a, b in zip(carry, q + p))

    state = lax.fori_loop(1, ring, rise, tuple(q + p))
    packed = pack(rows, list(state[:VREGS]), list(state[VREGS:]), 0)
    for v in range(VREGS):
        xin[x, pl.ds(v * 8, 8), :] = packed[v]
    xs = []
    for k in range(1, nx):
        c = send(xin.at[x], xin.at[x], x_s.at[k], x_r.at[k], x_dev(k))
        c.start()
        xs.append(c)

    for k in range(1, nx):
        mxs[k - 1].wait()
        there = lax.rem(x + nx - k, nx)
        src = maps.at[there, :, lanes(core)]
        c = send(src, src, mp_s.at[k], mp_r.at[k], mate)
        c.start()
        mps.append(c)
    for c in mps:
        c.wait()

    def mm(a, b):
        return jnp.dot(a, b, precision=lax.Precision.HIGHEST, preferred_element_type=F32)

    pad = jnp.zeros((256 - STATES, 128), F32)

    row2 = lax.broadcasted_iota(jnp.int32, (256, 256), 0)
    col2 = lax.broadcasted_iota(jnp.int32, (256, 256), 1)
    prefix[0] = jnp.where(row2 == col2, F32(1.0), F32(0.0))
    for i in range(nx):
        prefix[i + 1, 0:STATES, :] = mm(maps[i], prefix[i])
        prefix[i + 1, STATES:256, :] = jnp.zeros((256 - STATES, 256), F32)

    for c in xs:
        c.wait()
    sums[0] = jnp.zeros((256, 128), F32)
    for i in range(nx):
        q, p = unpack(xin.at[i])
        b = jnp.concatenate(q + p, axis=0)
        if i:
            b = b + mm(maps[i], sums[i])
        sums[i + 1, 0:STATES, :] = b
        sums[i + 1, STATES:256, :] = pad

    zcopy = send(zout, zin, z_s.at[0], z_r.at[0], z_dev(1))
    start[...] = jnp.zeros_like(start)

    @pl.when(z > 0)
    def _():
        zcopy.wait_recv()
        q, p = unpack(zin)
        for v, a in enumerate(q + p):
            start[pl.ds(v * 8, 8), :] = a

    @pl.when(z < nz - 1)
    def _():
        s = mm(prefix[nx, 0:STATES, :], start[...]) + sums[nx, 0:STATES, :]
        q = [s[v * 8 : v * 8 + 8] for v in range(VREGS)]
        p = [s[SIDE + v * 8 : SIDE + v * 8 + 8] for v in range(VREGS)]
        for v, a in enumerate(pack(rows, q, p, 0)):
            zout[pl.ds(v * 8, 8), :] = a
        zcopy.start()
        zcopy.wait_send()

    start[0:STATES, :] = mm(prefix[x, 0:STATES, :], start[...]) + sums[x, 0:STATES, :]

    q, p = load_state(start)

    def put(carry, j):
        for v, a in enumerate(pack(rows, list(carry[:VREGS]), list(carry[VREGS:]), 0)):
            sout[j, pl.ds(v * 8, 8), :] = a

    put(tuple(q + p), 0)

    def fall(j, carry):
        carry = block_free(carry, j)
        q, p = unpack(bin_.at[j])
        carry = tuple(a + b for a, b in zip(carry, q + p))
        put(carry, j + 1)
        return carry

    lax.fori_loop(0, ring - 1, fall, tuple(q + p))
    downs = []
    for k in range(1, ring):
        peer = lax.rem(r + k, ring)
        c = send(sout.at[peer], sin.at[r], dn_s.at[k], dn_r.at[k], ring_dev(k))
        c.start()
        downs.append(c)
    own = pltpu.make_async_copy(sout.at[r], sin.at[r], loc_sem.at[3])
    own.start()
    for c in downs:
        c.wait()
    own.wait()

    stores = []
    power_rows = []
    for f in range(tiles):
        a = [sin[2 * f, pl.ds(v * 8, 8), :] for v in range(VREGS)]
        b = [sin[2 * f + 1, pl.ds(v * 8, 8), :] for v in range(VREGS)]
        q = [jnp.where(rows.low, i, pltpu.roll(j, 64, 1)) for i, j in zip(a, b)]
        p = [jnp.where(rows.low, pltpu.roll(i, 64, 1), j) for i, j in zip(a, b)]
        q0, p0 = load_state(x0b.at[:, pl.ds(f * 128, 128)])
        q, p = [a + b for a, b in zip(q, q0)], [a + b for a, b in zip(p, p0)]

        def one(t, carry, f=f):
            q, p = list(carry[:VREGS]), list(carry[VREGS : 2 * VREGS])
            q, p = leap(rows, q, p, own_w(t))
            o = obs_ref[t].astype(F32)
            new = []
            squares = []
            for v, pred in enumerate(q + p):
                inn = mb[f, t, pl.ds(v * 8, 8), :] - pred
                squares.append(inn * inn)
                state = pred + (o * gain_rows[pl.ds(v * 8, 8), :]) * inn
                mb[f, t, pl.ds(v * 8, 8), :] = state
                new.append(state)
            while len(squares) > 1:
                squares = [a + b for a, b in zip(squares[::2], squares[1::2])] + (
                    [squares[-1]] if len(squares) % 2 else []
                )
            return (*new, carry[-1] + o * squares[0])

        state = lax.fori_loop(0, here, one, (*q, *p, rows.zero))
        power_rows.append(jnp.sum(state[-1], axis=0, keepdims=True))
        c = pltpu.make_async_copy(mb.at[f], out_hbm.at[:, :, pl.ds(f * 128, 128)], out_sem.at[f])
        c.start()
        stores.append(c)

    power = jnp.concatenate(power_rows + [jnp.zeros((8 - tiles, 128), F32)], axis=0)
    slot = 0
    for count, place, device in ((ring, r, ring_dev), (nx, x, x_dev), (nz, z, z_dev)):
        powers[slot + place] = power
        copies = []
        for k in range(1, count):
            ref = powers.at[slot + place]
            c = send(ref, ref, pw_s.at[slot + k], pw_r.at[slot + k], device(k))
            c.start()
            copies.append(c)
        for c in copies:
            c.wait()
        power = powers[slot]
        for k in range(1, count):
            power = power + powers[slot + k]
        slot += count
    total_steps = here * ring * nx * nz
    power_ref[...] = power[0:tiles] / F32(total_steps * STATES)
    for c in stores:
        c.wait()


def local(dims, measurements, observed, segment_ids, courant_table, filter_gains, initial_state):
    here, _, runs = measurements.shape
    nz, nx, ny = dims
    ring = ny * CORES
    tiles = runs // 128
    gains = jnp.pad(filter_gains, (0, 256 - STATES)).reshape(1, 256)
    smem = pl.BlockSpec(memory_space=pltpu.SMEM)
    vmem = pl.BlockSpec(memory_space=pltpu.VMEM)
    hbm = pl.BlockSpec(memory_space=pl.ANY)
    dma = pltpu.SemaphoreType.DMA
    packed = (SIDE, 128)
    filtered, power = pl.pallas_call(
        functools.partial(kernel, dims, runs, here),
        out_shape=(
            jax.ShapeDtypeStruct(measurements.shape, F32),
            jax.ShapeDtypeStruct((tiles, 128), F32),
        ),
        in_specs=[smem, smem, smem, vmem, hbm, hbm],
        out_specs=(hbm, vmem),
        scratch_shapes=[
            pltpu.VMEM((tiles, here, STATES, 128), F32),
            pltpu.VMEM((STATES, runs), F32),
            pltpu.VMEM((STATES, 128), F32),
            pltpu.VMEM((2, STATES, 128), F32),
            pltpu.VMEM((ring, 8, 128), jnp.int32),
            pltpu.SMEM((ring, 8, 128), jnp.int32),
            pltpu.VMEM((ring, *packed), F32),
            pltpu.VMEM((ring, *packed), F32),
            pltpu.VMEM((nx, STATES, 256), F32),
            pltpu.VMEM((nx + 1, 256, 256), F32),
            pltpu.VMEM((nx, *packed), F32),
            pltpu.VMEM((nx + 1, 256, 128), F32),
            pltpu.VMEM(packed, F32),
            pltpu.VMEM(packed, F32),
            pltpu.VMEM((256, 128), F32),
            pltpu.VMEM((ring, *packed), F32),
            pltpu.VMEM((ring, *packed), F32),
            pltpu.VMEM((ring + nx + nz, 8, 128), F32),
            dma((tiles,)),
            dma((tiles,)),
            dma((4,)),
            dma((ring,)),
            dma((ring,)),
            dma((ring,)),
            dma((ring,)),
            dma((nx,)),
            dma((nx,)),
            dma((nx,)),
            dma((nx,)),
            dma((nx,)),
            dma((nx,)),
            dma((1,)),
            dma((1,)),
            dma((ring,)),
            dma((ring,)),
            dma((ring + nx + nz,)),
            dma((ring + nx + nz,)),
        ],
        compiler_params=pltpu.CompilerParams(
            collective_id=0, has_side_effects=True, vmem_limit_bytes=48 << 20
        ),
    )(segment_ids, observed, courant_table, gains, measurements, initial_state)
    return filtered, power.reshape(runs)


def solution(mesh):
    dims = torus_of(mesh.size)
    in_specs = (P("tm", None, None), P("tm"), P("tm"), P(), P(), P())
    out_specs = (P("tm", None, None), P())
    return jax.shard_map(
        functools.partial(local, dims), mesh=mesh, in_specs=in_specs, out_specs=out_specs, check_vma=False
    )
```

time: 770 us -> 64.6 us (0.08)
  blocking collectives: 439 us -> 0 us
  waiting for transfers between devices: 233 us -> 0 us
  Pallas kernels: 0 us -> 57.8 us
  matrix products: 41.7 us -> 0 us
  other arithmetic: 26.6 us -> 0 us
  between operations: 14.2 us -> 0.64 us
    psum x1 -> x0, blocking collectives: 439 us -> none  [local(): total_power = lax.psum(partial_power, 'tm')]
    all_gather x2 -> x0, waiting for transfers between devices: 232 us -> none  [prefix(): gathered = jax.tree.map(lambda a: lax.all_gather(a, axis), part)]
    pallas_call x0 -> x1, Pallas kernels: none -> 57.8 us  [local(): pl.pallas_call(functools.partial(kernel, dims, runs, here), out_shape=(ja...]
    dot_general x28 -> x0, matrix products: 41.7 us -> none  [the longest x25 39 us: matmul(): jnp.dot(left, right, precision=HIGHEST, preferred_element_type=jnp.float32)]
    mul x18 -> x0, other arithmetic: 14.6 us -> none  [the longest x8 4.98 us: advance(): updated = predicted + weight * filter_gains[:, None] * innovation]
    reduce_sum x9 -> x0, other arithmetic: 8.75 us -> none  [the longest x8 8.73 us: advance(): power = weight * jnp.sum(innovation * innovation, axis=0)]
  transfers between devices with their start and end apart: 2 -> 0, of which waited for: 2 -> 0; matrix products, arithmetic and copies ran while one was open for 0% -> 0% of each run, Pallas kernels for 0% -> 0%
where the time goes in v1:
time: 64.6 us; the launch traced here: 64.4 us
  Pallas kernels  57.8 us (89%)
  local copies, waits for them, and re-layouts  6 us (9%)
    pallas_call x1, Pallas kernels, local(): pl.pallas_call(functools.partial(kernel, dims, runs, here), out_shape=(ja...  57.8 us
    unnamed x9, local copies, waits for them, and re-layouts  5.31 us

profile of v1, /device:TPU:0, one launch (start us, length us, event | category | flops | bytes accessed | tf_op | source)
XLA Modules:
  0.0 64.4 jit_solution(16124205034167751628)
XLA Ops:
  0.6 0.7 %pad.4 = f32[256]{0:T(256)S(1)} pad(f32[192]{0:T(256)} %param.10, f32[]{:T(128)} %constant.2.clone.1), padding=0_64 | pad | bytes 1796 | tf_op jit(solution)/shard_map/jit(_pad)/pad | solution.py:395
  1.3 0.8 %copy.8.table_ref = f32[32,4]{1,0:T(8,128)S(1)} copy(f32[32,4]{0,1:T(4,128)} %param.9) | data formatting | bytes 1024 | tf_op args[3]
  2.1 0.0 copy-start
  2.1 1.0 %copy-done = f32[192,512]{1,0:T(8,128)S(1)} copy-done((f32[192,512]{1,0:T(8,128)S(1)}, f32[192,512]{1,0:T(8,128)}, u32[]{:S(2)}) %copy-start) | copy-done | bytes 393240
  3.1 0.0 copy-start.1
  3.1 0.7 %copy-done.1 = s32[8]{0:T(128)S(1)} copy-done((s32[8]{0:T(128)S(1)}, s32[8]{0:T(128)}, u32[]{:S(2)}) %copy-start.1) | copy-done | bytes 56
  3.7 0.0 copy-start.2
  3.7 0.7 %copy-done.2 = s32[8]{0:T(128)S(1)} copy-done((s32[8]{0:T(128)S(1)}, s32[8]{0:T(128)}, u32[]{:S(2)}) %copy-start.2) | copy-done | bytes 56
  4.4 57.8 %shard_map.77 = (f32[8,192,512]{2,1,0:T(8,128)S(1)}, f32[4,128]{1,0:T(4,128)S(1)}) custom-call(s32[8]{0:T(128)S(1)} %copy-done.1, s32[8]{0:T(128)S(1)} %copy-done.2, f32[32,4]{1,0:T(8,128)S(1)} %copy.8.table_ref, f32[1,256]{1,0:T(1,128)S(1)} %bitcast.2, f32[8,192,512]{2,1,0:T(8,128)} %m_hbm.1, f32[192,512]{1,0:T(8,128)S(1)} %copy-done), custom_call_target="tpu_custom_call" | custom-call | tf_op jit(solution)/shard_map/pallas_call | solution.py:401
  62.2 1.7 %copy.11 = f32[8,192,512]{2,1,0:T(8,128)} copy(f32[8,192,512]{2,1,0:T(8,128)S(1)} %get-tuple-element.8) | data formatting | bytes 6291456
  63.9 0.6 copy.12
Async XLA Ops:
  2.1 1.0 %copy-start = (f32[192,512]{1,0:T(8,128)S(1)}, f32[192,512]{1,0:T(8,128)}, u32[]{:S(2)}) copy-start(f32[192,512]{1,0:T(8,128)} %x0_hbm.1) | copy-start | bytes 1179652
  3.1 0.7 %copy-start.1 = (s32[8]{0:T(128)S(1)}, s32[8]{0:T(128)}, u32[]{:S(2)}) copy-start(s32[8]{0:T(128)} %seg_ref.1) | copy-start | bytes 100
  3.7 0.7 %copy-start.2 = (s32[8]{0:T(128)S(1)}, s32[8]{0:T(128)}, u32[]{:S(2)}) copy-start(s32[8]{0:T(128)} %obs_ref.1) | copy-start | bytes 100

commit v2 on v1

--- a/solution.py
+++ b/solution.py
@@ -37,23 +37,25 @@
         self.low = lax.broadcasted_iota(jnp.int32, (8, 128), 1) < 64
 
 
+def node(v):
+    return pl.ds(HALF * (v // 3) + v % 3, 8, stride=3)
+
+
 def leap(rows, q, p, w):
-    rolled = [pltpu.roll(v, 1, 0) for v in q]
     total = (q[2] + q[5]) + (q[8] + q[11])
+    wrap = [jnp.where(rows.first, rows.zero, pltpu.roll(q[3 * c + 2], 1, 0)) for c in range(CABLES)]
     new_p, u = [], []
     for v in range(VREGS):
-        before = jnp.where(rows.first, rolled[v - 1] if v % 3 else rows.zero, rolled[v])
-        d = q[v] - before
+        d = q[v] - (q[v - 1] if v % 3 else wrap[v // 3])
         if v % 3 == 2:
             d = d - rows.pay * (total - q[v])
         new_p.append(p[v] + w[v // 3] * d)
         u.append(w[v // 3] * new_p[v])
-    rolled = [pltpu.roll(v, 7, 0) for v in u]
+    wrap = [jnp.where(rows.last, rows.zero, pltpu.roll(u[3 * c], 7, 0)) for c in range(CABLES)]
     total = (u[2] + u[5]) + (u[8] + u[11])
     new_q = []
     for v in range(VREGS):
-        after = jnp.where(rows.last, rolled[v + 1] if v % 3 < 2 else rows.zero, rolled[v])
-        e = u[v] - after
+        e = u[v] - (u[v + 1] if v % 3 < 2 else wrap[v // 3])
         if v % 3 == 2:
             e = e - rows.pay * (total - u[v])
         new_q.append(q[v] - e)
@@ -70,10 +72,10 @@
     dims, runs, steps,
     seg_ref, obs_ref, table_ref, gains_ref, m_hbm, x0_hbm,
     out_hbm, power_ref,
-    mb, x0b, gain_rows, keep, params_v, params_s, bpack, bin_, maps, prefix, xin, sums, zin, zout,
+    mb, x0b, tab, phi, phi_out, starts, firsts, gain_rows, keep, params_v, params_s, bpack, bin_, maps, prefix, xin, sums, zin, zout,
     start, sout, sin, powers,
     m_sem, out_sem, loc_sem,
-    par_s, par_r, up_s, up_r, mx_s, mx_r, mp_s, mp_r, x_s, x_r, z_s, z_r, dn_s, dn_r, pw_s, pw_r,
+    par_s, par_r, up_s, up_r, mx_s, mx_r, mp_s, mp_r, x_s, x_r, z_s, z_r, dn_s, dn_r, st_s, st_r, ph_s, ph_r, pw_s, pw_r,
 ):
     nz, nx, ny = dims
     ring = ny * CORES
@@ -117,9 +119,13 @@
 
     @pl.when(me == 0)
     def _():
-        c = pltpu.make_async_copy(x0_hbm, x0b, loc_sem.at[0])
-        c.start()
-        c.wait()
+        copies = []
+        for f in range(tiles):
+            c = pltpu.make_async_copy(x0_hbm.at[:, pl.ds(f * 128, 128)], x0b.at[f], loc_sem.at[0])
+            c.start()
+            copies.append(c)
+        for c in copies:
+            c.wait()
 
     @pl.when(me > 0)
     def _():
@@ -138,13 +144,19 @@
         for part in range(2):
             g = jnp.broadcast_to(gains_ref[0:1, part * 128 : part * 128 + 128], (8, 128))
             spread = spread + jnp.sum(
-                jnp.where(lane_i + part * 128 == row_i + v * 8, g, F32(0.0)), axis=1, keepdims=True
+                jnp.where(lane_i + part * 128 == row_i * 3 + (HALF * (v // 3) + v % 3), g, F32(0.0)), axis=1, keepdims=True
             )
         g = jnp.broadcast_to(spread, (8, 128))
         gain_rows[pl.ds(v * 8, 8), :] = g
         keep[0, pl.ds(v * 8, 8), :] = jnp.ones((8, 128), F32)
         keep[1, pl.ds(v * 8, 8), :] = 1.0 - g
 
+    for c in range(CABLES):
+        tab[c] = jnp.broadcast_to(table_ref[:, c : c + 1], (SEGS, 128))
+
+    def spread_w(s):
+        return [jnp.broadcast_to(tab[c, pl.ds(s, 1), :], (8, 128)) for c in range(CABLES)]
+
     pl.semaphore_wait(barrier, (ring - 1) + (nx - 1) + (nz - 1))
 
     par = []
@@ -159,9 +171,14 @@
             [ref_q[pl.ds(SIDE + v * 8, 8), :] for v in range(VREGS)],
         )
 
+    def load_first(f):
+        return (
+            [x0b[f, node(v), :] for v in range(VREGS)],
+            [x0b[f, node(VREGS + v), :] for v in range(VREGS)],
+        )
+
     def own_w(t):
-        s = seg_ref[t]
-        return [table_ref[s, c] for c in range(CABLES)]
+        return spread_w(seg_ref[t])
 
     ups = {}
     for f in range(tiles):
@@ -173,12 +190,12 @@
             o = obs_ref[t].astype(F32)
             new = []
             for v, pred in enumerate(q + p):
-                inn = mb[f, t, pl.ds(v * 8, 8), :] - pred
+                inn = mb[f, t, node(v), :] - pred
                 new.append(pred + (o * gain_rows[pl.ds(v * 8, 8), :]) * inn)
             return tuple(new)
 
-        q, p = load_state(x0b.at[:, pl.ds(f * 128, 128)])
-        state = lax.fori_loop(0, here, one, tuple(q + p))
+        q, p = load_first(f)
+        state = lax.fori_loop(0, here, one, tuple(q + p), unroll=2)
         q, p = list(state[:VREGS]), list(state[VREGS:])
         for half in range(2):
             packed = pack(rows, q, p, half)
@@ -202,19 +219,34 @@
         q, p = list(carry[:VREGS]), list(carry[VREGS:])
         s = params_s[j, 0, t]
         o = params_s[j, 1, t]
-        q, p = leap(rows, q, p, [table_ref[s, c] for c in range(CABLES)])
+        q, p = leap(rows, q, p, spread_w(s))
         return tuple(a * keep[o, pl.ds(v * 8, 8), :] for v, a in enumerate(q + p))
 
     def block_free(carry, j):
-        return lax.fori_loop(0, here, lambda t, s: step_free(s, j, t), carry)
+        return lax.fori_loop(0, here, lambda t, s: step_free(s, j, t), carry, unroll=4)
 
     col = lane_i + core * 128
     state = tuple(jnp.where(col == row_i + v * 8, F32(1.0), F32(0.0)) for v in range(2 * VREGS))
-    state = lax.fori_loop(0, ring, lambda j, s: block_free(s, j), state)
+    mate = me + 1 - 2 * core
+    mate_r = r + 1 - 2 * core
+
+    def climb(j, carry):
+        @pl.when(j == r)
+        def _():
+            for v, a in enumerate(carry):
+                phi[pl.ds(v * 8, 8), lanes(core)] = a
+
+        @pl.when(j == mate_r)
+        def _():
+            for v, a in enumerate(carry):
+                phi_out[pl.ds(v * 8, 8), :] = a
+
+        return block_free(carry, j)
+
+    state = lax.fori_loop(0, ring, climb, state)
     for v in range(2 * VREGS):
         maps[x, pl.ds(v * 8, 8), lanes(core)] = state[v]
     mine = maps.at[x, :, lanes(core)]
-    mate = me + 1 - 2 * core
     mxs = []
     for k in range(1, nx):
         c = send(mine, mine, mx_s.at[k], mx_r.at[k], x_dev(k))
@@ -223,6 +255,9 @@
     mps = [send(mine, mine, mp_s.at[0], mp_r.at[0], mate)]
     mps[0].start()
 
+    phic = send(phi_out, phi.at[:, lanes(core)], ph_s.at[0], ph_r.at[0], mate)
+    phic.start()
+
     for k in range(1, ring):
         ups[k].wait()
     own.wait()
@@ -231,9 +266,16 @@
         a = [ref[pl.ds(v * 8, 8), :] for v in range(VREGS)]
         return a, [pltpu.roll(v, 64, 1) for v in a]
 
+    def put(carry, j):
+        for v, a in enumerate(pack(rows, list(carry[:VREGS]), list(carry[VREGS:]), 0)):
+            sout[j, pl.ds(v * 8, 8), :] = a
+
+    for v in range(VREGS):
+        sout[0, pl.ds(v * 8, 8), :] = rows.zero
     q, p = unpack(bin_.at[0])
 
     def rise(j, carry):
+        put(carry, j)
         carry = block_free(carry, j)
         q, p = unpack(bin_.at[j])
         return tuple(a + b for a, b in zip(carry, q + p))
@@ -247,6 +289,15 @@
         c = send(xin.at[x], xin.at[x], x_s.at[k], x_r.at[k], x_dev(k))
         c.start()
         xs.append(c)
+
+    downs = []
+    for k in range(1, ring):
+        peer = lax.rem(r + k, ring)
+        c = send(sout.at[peer], sin.at[r], dn_s.at[k], dn_r.at[k], ring_dev(k))
+        c.start()
+        downs.append(c)
+    own_down = pltpu.make_async_copy(sout.at[r], sin.at[r], loc_sem.at[3])
+    own_down.start()
 
     for k in range(1, nx):
         mxs[k - 1].wait()
@@ -304,41 +355,41 @@
     start[0:STATES, :] = mm(prefix[x, 0:STATES, :], start[...]) + sums[x, 0:STATES, :]
 
     q, p = load_state(start)
-
-    def put(carry, j):
-        for v, a in enumerate(pack(rows, list(carry[:VREGS]), list(carry[VREGS:]), 0)):
-            sout[j, pl.ds(v * 8, 8), :] = a
-
-    put(tuple(q + p), 0)
-
-    def fall(j, carry):
-        carry = block_free(carry, j)
-        q, p = unpack(bin_.at[j])
-        carry = tuple(a + b for a, b in zip(carry, q + p))
-        put(carry, j + 1)
-        return carry
-
-    lax.fori_loop(0, ring - 1, fall, tuple(q + p))
-    downs = []
+    for v, a in enumerate(pack(rows, q, p, 0)):
+        starts[r, pl.ds(v * 8, 8), :] = a
+    sts = []
     for k in range(1, ring):
-        peer = lax.rem(r + k, ring)
-        c = send(sout.at[peer], sin.at[r], dn_s.at[k], dn_r.at[k], ring_dev(k))
-        c.start()
-        downs.append(c)
-    own = pltpu.make_async_copy(sout.at[r], sin.at[r], loc_sem.at[3])
-    own.start()
+        c = send(starts.at[r], starts.at[r], st_s.at[k], st_r.at[k], ring_dev(k))
+        c.start()
+        sts.append(c)
+    phic.wait()
     for c in downs:
         c.wait()
-    own.wait()
+    own_down.wait()
+    for c in sts:
+        c.wait()
+
+    def merge(ref, f):
+        a = [ref[2 * f, pl.ds(v * 8, 8), :] for v in range(VREGS)]
+        b = [ref[2 * f + 1, pl.ds(v * 8, 8), :] for v in range(VREGS)]
+        q = [jnp.where(rows.low, i, pltpu.roll(j, 64, 1)) for i, j in zip(a, b)]
+        p = [jnp.where(rows.low, pltpu.roll(i, 64, 1), j) for i, j in zip(a, b)]
+        return q, p
+
+    for f in range(tiles):
+        q, p = merge(starts, f)
+        for v, a in enumerate(q + p):
+            firsts[pl.ds(v * 8, 8), pl.ds(f * 128, 128)] = a
+    firsts[STATES:256, :] = jnp.zeros((256 - STATES, runs), F32)
+    firsts[0:STATES, :] = mm(phi[...], firsts[...])
 
     stores = []
     power_rows = []
     for f in range(tiles):
-        a = [sin[2 * f, pl.ds(v * 8, 8), :] for v in range(VREGS)]
-        b = [sin[2 * f + 1, pl.ds(v * 8, 8), :] for v in range(VREGS)]
-        q = [jnp.where(rows.low, i, pltpu.roll(j, 64, 1)) for i, j in zip(a, b)]
-        p = [jnp.where(rows.low, pltpu.roll(i, 64, 1), j) for i, j in zip(a, b)]
-        q0, p0 = load_state(x0b.at[:, pl.ds(f * 128, 128)])
+        q, p = merge(sin, f)
+        q1, p1 = load_state(firsts.at[:, pl.ds(f * 128, 128)])
+        q, p = [a + b for a, b in zip(q, q1)], [a + b for a, b in zip(p, p1)]
+        q0, p0 = load_first(f)
         q, p = [a + b for a, b in zip(q, q0)], [a + b for a, b in zip(p, p0)]
 
         def one(t, carry, f=f):
@@ -348,10 +399,10 @@
             new = []
             squares = []
             for v, pred in enumerate(q + p):
-                inn = mb[f, t, pl.ds(v * 8, 8), :] - pred
+                inn = mb[f, t, node(v), :] - pred
                 squares.append(inn * inn)
                 state = pred + (o * gain_rows[pl.ds(v * 8, 8), :]) * inn
-                mb[f, t, pl.ds(v * 8, 8), :] = state
+                mb[f, t, node(v), :] = state
                 new.append(state)
             while len(squares) > 1:
                 squares = [a + b for a, b in zip(squares[::2], squares[1::2])] + (
@@ -359,7 +410,7 @@
                 )
             return (*new, carry[-1] + o * squares[0])
 
-        state = lax.fori_loop(0, here, one, (*q, *p, rows.zero))
+        state = lax.fori_loop(0, here, one, (*q, *p, rows.zero), unroll=2)
         power_rows.append(jnp.sum(state[-1], axis=0, keepdims=True))
         c = pltpu.make_async_copy(mb.at[f], out_hbm.at[:, :, pl.ds(f * 128, 128)], out_sem.at[f])
         c.start()
@@ -404,11 +455,16 @@
             jax.ShapeDtypeStruct(measurements.shape, F32),
             jax.ShapeDtypeStruct((tiles, 128), F32),
         ),
-        in_specs=[smem, smem, smem, vmem, hbm, hbm],
+        in_specs=[smem, smem, vmem, vmem, hbm, hbm],
         out_specs=(hbm, vmem),
         scratch_shapes=[
             pltpu.VMEM((tiles, here, STATES, 128), F32),
-            pltpu.VMEM((STATES, runs), F32),
+            pltpu.VMEM((tiles, STATES, 128), F32),
+            pltpu.VMEM((CABLES, SEGS, 128), F32),
+            pltpu.VMEM((STATES, 256), F32),
+            pltpu.VMEM((STATES, 128), F32),
+            pltpu.VMEM((ring, *packed), F32),
+            pltpu.VMEM((256, runs), F32),
             pltpu.VMEM((STATES, 128), F32),
             pltpu.VMEM((2, STATES, 128), F32),
             pltpu.VMEM((ring, 8, 128), jnp.int32),
@@ -442,6 +498,10 @@
             dma((1,)),
             dma((ring,)),
             dma((ring,)),
+            dma((ring,)),
+            dma((ring,)),
+            dma((1,)),
+            dma((1,)),
             dma((ring + nx + nz,)),
             dma((ring + nx + nz,)),
         ],

time: 64.6 us -> 60.9 us (0.943)
  Pallas kernels: 57.8 us -> 54.1 us
    pallas_call x1, Pallas kernels: 57.8 us -> 54.1 us  [local(): pl.pallas_call(functools.partial(kernel, dims, runs, here), out_shape=(ja...]
where the time goes in v2:
time: 60.9 us; the launch traced here: 60.7 us
  Pallas kernels  54.1 us (89%)
  local copies, waits for them, and re-layouts  6 us (10%)
  between operations  0.64 us (1%)
    pallas_call x1, Pallas kernels, local(): pl.pallas_call(functools.partial(kernel, dims, runs, here), out_shape=(ja...  54.1 us
    unnamed x9, local copies, waits for them, and re-layouts  5.31 us

profile of v2, /device:TPU:0, one launch (start us, length us, event | category | flops | bytes accessed | tf_op | source)
XLA Modules:
  0.0 60.7 jit_solution(13829683590552299930)
XLA Ops:
  0.6 0.7 %pad.4 = f32[256]{0:T(256)S(1)} pad(f32[192]{0:T(256)} %param.10, f32[]{:T(128)} %constant.2.clone.1), padding=0_64 | pad | bytes 1796 | tf_op jit(solution)/shard_map/jit(_pad)/pad | solution.py:446
  1.3 0.8 %copy.8.table_ref = f32[32,4]{1,0:T(8,128)S(1)} copy(f32[32,4]{0,1:T(4,128)} %param.9) | data formatting | bytes 1024 | tf_op args[3]
  2.1 0.0 copy-start
  2.1 1.0 %copy-done = f32[192,512]{1,0:T(8,128)S(1)} copy-done((f32[192,512]{1,0:T(8,128)S(1)}, f32[192,512]{1,0:T(8,128)}, u32[]{:S(2)}) %copy-start) | copy-done | bytes 393240
  3.1 0.0 copy-start.1
  3.1 0.7 %copy-done.1 = s32[8]{0:T(128)S(1)} copy-done((s32[8]{0:T(128)S(1)}, s32[8]{0:T(128)}, u32[]{:S(2)}) %copy-start.1) | copy-done | bytes 56
  3.7 0.0 copy-start.2
  3.7 0.7 %copy-done.2 = s32[8]{0:T(128)S(1)} copy-done((s32[8]{0:T(128)S(1)}, s32[8]{0:T(128)}, u32[]{:S(2)}) %copy-start.2) | copy-done | bytes 56
  4.4 54.1 %shard_map.77 = (f32[8,192,512]{2,1,0:T(8,128)S(1)}, f32[4,128]{1,0:T(4,128)S(1)}) custom-call(s32[8]{0:T(128)S(1)} %copy-done.1, s32[8]{0:T(128)S(1)} %copy-done.2, f32[32,4]{1,0:T(8,128)S(1)} %copy.8.table_ref, f32[1,256]{1,0:T(1,128)S(1)} %bitcast.2, f32[8,192,512]{2,1,0:T(8,128)} %m_hbm.1, f32[192,512]{1,0:T(8,128)S(1)} %copy-done), custom_call_target="tpu_custom_call" | custom-call | tf_op jit(solution)/shard_map/pallas_call | solution.py:452
  58.5 1.7 %copy.11 = f32[8,192,512]{2,1,0:T(8,128)} copy(f32[8,192,512]{2,1,0:T(8,128)S(1)} %get-tuple-element.8) | data formatting | bytes 6291456
  60.1 0.6 copy.12
Async XLA Ops:
  2.1 1.0 %copy-start = (f32[192,512]{1,0:T(8,128)S(1)}, f32[192,512]{1,0:T(8,128)}, u32[]{:S(2)}) copy-start(f32[192,512]{1,0:T(8,128)} %x0_hbm.1) | copy-start | bytes 1179652
  3.1 0.7 %copy-start.1 = (s32[8]{0:T(128)S(1)}, s32[8]{0:T(128)}, u32[]{:S(2)}) copy-start(s32[8]{0:T(128)} %seg_ref.1) | copy-start | bytes 100
  3.7 0.7 %copy-start.2 = (s32[8]{0:T(128)S(1)}, s32[8]{0:T(128)}, u32[]{:S(2)}) copy-start(s32[8]{0:T(128)} %obs_ref.1) | copy-start | bytes 100

commit v3 on v2

--- a/solution.py
+++ b/solution.py
@@ -70,9 +70,9 @@
 
 def kernel(
     dims, runs, steps,
-    seg_ref, obs_ref, table_ref, gains_ref, m_hbm, x0_hbm,
+    seg_hbm, obs_hbm, table_hbm, gains_hbm, m_hbm, x0_hbm,
     out_hbm, power_ref,
-    mb, x0b, tab, phi, phi_out, starts, firsts, gain_rows, keep, params_v, params_s, bpack, bin_, maps, prefix, xin, sums, zin, zout,
+    seg_ref, obs_ref, table_ref, gains_ref, small_sem, mb, x0b, tab, phi, phi_out, starts, firsts, gain_rows, keep, params_v, params_s, bpack, bin_, maps, prefix, xin, sums, zin, zout,
     start, sout, sin, powers,
     m_sem, out_sem, loc_sem,
     par_s, par_r, up_s, up_r, mx_s, mx_r, mp_s, mp_r, x_s, x_r, z_s, z_r, dn_s, dn_r, st_s, st_r, ph_s, ph_r, pw_s, pw_r,
@@ -103,6 +103,13 @@
             src_ref=src, dst_ref=dst, send_sem=ssem, recv_sem=rsem, device_id=(dev,), device_id_type=MESH
         )
 
+    smalls = []
+    for i, (src, dst) in enumerate(
+        ((seg_hbm, seg_ref), (obs_hbm, obs_ref), (table_hbm, table_ref), (gains_hbm, gains_ref))
+    ):
+        c = pltpu.make_async_copy(src, dst, small_sem.at[i])
+        c.start()
+        smalls.append(c)
     loads = []
     for f in range(tiles):
         c = pltpu.make_async_copy(m_hbm.at[:, :, pl.ds(f * 128, 128)], mb.at[f], m_sem.at[f])
@@ -131,6 +138,9 @@
     def _():
         x0b[...] = jnp.zeros_like(x0b)
 
+    for c in smalls:
+        c.wait()
+
     row_i = lax.broadcasted_iota(jnp.int32, (8, 128), 0)
     lane_i = lax.broadcasted_iota(jnp.int32, (8, 128), 1)
     tile = jnp.zeros((8, 128), jnp.int32)
@@ -139,10 +149,14 @@
         tile = jnp.where((row_i == 1) & (lane_i == t), obs_ref[t], tile)
     params_v[r] = tile
 
+    gain_lanes = [
+        gains_ref[0:1, 0:128],
+        jnp.concatenate([gains_ref[0:1, 128:STATES], jnp.zeros((1, 256 - STATES), F32)], axis=1),
+    ]
     for v in range(STATES // 8):
         spread = jnp.zeros((8, 1), F32)
         for part in range(2):
-            g = jnp.broadcast_to(gains_ref[0:1, part * 128 : part * 128 + 128], (8, 128))
+            g = jnp.broadcast_to(gain_lanes[part], (8, 128))
             spread = spread + jnp.sum(
                 jnp.where(lane_i + part * 128 == row_i * 3 + (HALF * (v // 3) + v % 3), g, F32(0.0)), axis=1, keepdims=True
             )
@@ -181,26 +195,34 @@
         return spread_w(seg_ref[t])
 
     ups = {}
-    for f in range(tiles):
-        loads[f].wait()
-
-        def one(t, carry, f=f):
-            q, p = list(carry[:VREGS]), list(carry[VREGS:])
-            q, p = leap(rows, q, p, own_w(t))
+    both = 2 * VREGS
+    for f0 in range(0, tiles, 2):
+        loads[f0].wait()
+        loads[f0 + 1].wait()
+
+        def one(t, carry, f0=f0):
+            w = own_w(t)
             o = obs_ref[t].astype(F32)
-            new = []
-            for v, pred in enumerate(q + p):
-                inn = mb[f, t, node(v), :] - pred
-                new.append(pred + (o * gain_rows[pl.ds(v * 8, 8), :]) * inn)
+            preds = []
+            for i in range(2):
+                s = list(carry[i * both : (i + 1) * both])
+                preds.append(leap(rows, s[:VREGS], s[VREGS:], w))
+            new = [None] * (2 * both)
+            for v in range(both):
+                gain = o * gain_rows[pl.ds(v * 8, 8), :]
+                for i, (q, p) in enumerate(preds):
+                    pred = (q + p)[v]
+                    new[i * both + v] = pred + gain * (mb[f0 + i, t, node(v), :] - pred)
             return tuple(new)
 
-        q, p = load_first(f)
-        state = lax.fori_loop(0, here, one, tuple(q + p), unroll=2)
-        q, p = list(state[:VREGS]), list(state[VREGS:])
-        for half in range(2):
-            packed = pack(rows, q, p, half)
-            for v in range(VREGS):
-                bpack[2 * f + half, pl.ds(v * 8, 8), :] = packed[v]
+        first = [load_first(f0), load_first(f0 + 1)]
+        state = lax.fori_loop(0, here, one, tuple(a for q, p in first for a in q + p), unroll=2)
+        for i in range(2):
+            s = list(state[i * both : (i + 1) * both])
+            for half in range(2):
+                packed = pack(rows, s[:VREGS], s[VREGS:], half)
+                for v in range(VREGS):
+                    bpack[2 * (f0 + i) + half, pl.ds(v * 8, 8), :] = packed[v]
     for k in range(1, ring):
         peer = lax.rem(r + k, ring)
         c = send(bpack.at[peer], bin_.at[r], up_s.at[k], up_r.at[k], ring_dev(k))
@@ -385,36 +407,45 @@
 
     stores = []
     power_rows = []
-    for f in range(tiles):
-        q, p = merge(sin, f)
-        q1, p1 = load_state(firsts.at[:, pl.ds(f * 128, 128)])
-        q, p = [a + b for a, b in zip(q, q1)], [a + b for a, b in zip(p, p1)]
-        q0, p0 = load_first(f)
-        q, p = [a + b for a, b in zip(q, q0)], [a + b for a, b in zip(p, p0)]
-
-        def one(t, carry, f=f):
-            q, p = list(carry[:VREGS]), list(carry[VREGS : 2 * VREGS])
-            q, p = leap(rows, q, p, own_w(t))
+    for f0 in range(0, tiles, 2):
+        first = []
+        for f in (f0, f0 + 1):
+            q, p = merge(sin, f)
+            q1, p1 = load_state(firsts.at[:, pl.ds(f * 128, 128)])
+            q0, p0 = load_first(f)
+            first += [a + b + c for a, b, c in zip(q + p, q1 + p1, q0 + p0)]
+
+        def one(t, carry, f0=f0):
+            w = own_w(t)
             o = obs_ref[t].astype(F32)
-            new = []
-            squares = []
-            for v, pred in enumerate(q + p):
-                inn = mb[f, t, node(v), :] - pred
-                squares.append(inn * inn)
-                state = pred + (o * gain_rows[pl.ds(v * 8, 8), :]) * inn
-                mb[f, t, node(v), :] = state
-                new.append(state)
-            while len(squares) > 1:
-                squares = [a + b for a, b in zip(squares[::2], squares[1::2])] + (
-                    [squares[-1]] if len(squares) % 2 else []
-                )
-            return (*new, carry[-1] + o * squares[0])
-
-        state = lax.fori_loop(0, here, one, (*q, *p, rows.zero), unroll=2)
-        power_rows.append(jnp.sum(state[-1], axis=0, keepdims=True))
-        c = pltpu.make_async_copy(mb.at[f], out_hbm.at[:, :, pl.ds(f * 128, 128)], out_sem.at[f])
-        c.start()
-        stores.append(c)
+            preds = []
+            for i in range(2):
+                s = list(carry[i * both : (i + 1) * both])
+                preds.append(leap(rows, s[:VREGS], s[VREGS:], w))
+            new = [None] * (2 * both)
+            square = [[rows.zero] * 4, [rows.zero] * 4]
+            for v in range(both):
+                gain = o * gain_rows[pl.ds(v * 8, 8), :]
+                for i, (q, p) in enumerate(preds):
+                    pred = (q + p)[v]
+                    inn = mb[f0 + i, t, node(v), :] - pred
+                    square[i][v % 4] = square[i][v % 4] + inn * inn
+                    state = pred + gain * inn
+                    mb[f0 + i, t, node(v), :] = state
+                    new[i * both + v] = state
+            out = [
+                carry[2 * both + i] + o * ((square[i][0] + square[i][1]) + (square[i][2] + square[i][3]))
+                for i in range(2)
+            ]
+            return (*new, *out)
+
+        state = lax.fori_loop(0, here, one, (*first, rows.zero, rows.zero), unroll=2)
+        for i in range(2):
+            power_rows.append(jnp.sum(state[2 * both + i], axis=0, keepdims=True))
+            f = f0 + i
+            c = pltpu.make_async_copy(mb.at[f], out_hbm.at[:, :, pl.ds(f * 128, 128)], out_sem.at[f])
+            c.start()
+            stores.append(c)
 
     power = jnp.concatenate(power_rows + [jnp.zeros((8 - tiles, 128), F32)], axis=0)
     slot = 0
@@ -443,8 +474,7 @@
     nz, nx, ny = dims
     ring = ny * CORES
     tiles = runs // 128
-    gains = jnp.pad(filter_gains, (0, 256 - STATES)).reshape(1, 256)
-    smem = pl.BlockSpec(memory_space=pltpu.SMEM)
+    gains = filter_gains.reshape(1, STATES)
     vmem = pl.BlockSpec(memory_space=pltpu.VMEM)
     hbm = pl.BlockSpec(memory_space=pl.ANY)
     dma = pltpu.SemaphoreType.DMA
@@ -455,9 +485,14 @@
             jax.ShapeDtypeStruct(measurements.shape, F32),
             jax.ShapeDtypeStruct((tiles, 128), F32),
         ),
-        in_specs=[smem, smem, vmem, vmem, hbm, hbm],
+        in_specs=[hbm] * 6,
         out_specs=(hbm, vmem),
         scratch_shapes=[
+            pltpu.SMEM((here,), jnp.int32),
+            pltpu.SMEM((here,), jnp.int32),
+            pltpu.VMEM((SEGS, CABLES), F32),
+            pltpu.VMEM((1, STATES), F32),
+            dma((4,)),
             pltpu.VMEM((tiles, here, STATES, 128), F32),
             pltpu.VMEM((tiles, STATES, 128), F32),
             pltpu.VMEM((CABLES, SEGS, 128), F32),

time: 60.9 us -> 60.4 us (level)
    pad x1 -> x0, local copies, waits for them, and re-layouts: 0.68 us -> none  [local(): gains = jnp.pad(filter_gains, (0, 256 - STATES)).reshape(1, 256)]
    unnamed x9 -> x11, local copies, waits for them, and re-layouts: 5.31 us -> 5.99 us
where the time goes in v3:
time: 60.4 us; the launch traced here: 60.2 us
  Pallas kernels  53.6 us (89%)
  local copies, waits for them, and re-layouts  5.99 us (10%)
  between operations  0.64 us (1%)
    pallas_call x1, Pallas kernels, local(): pl.pallas_call(functools.partial(kernel, dims, runs, here), out_shape=(ja...  53.6 us
    unnamed x11, local copies, waits for them, and re-layouts  5.99 us

profile of v3, /device:TPU:0, one launch (start us, length us, event | category | flops | bytes accessed | tf_op | source)
XLA Modules:
  0.0 60.2 jit_solution(8550282939756511127)
XLA Ops:
  0.6 0.8 %copy.8.table_hbm = f32[32,4]{1,0:T(8,128)S(1)} copy(f32[32,4]{0,1:T(4,128)} %param.9) | data formatting | bytes 1024 | tf_op args[3]
  1.4 0.0 copy-start
  1.4 1.0 %copy-done = f32[192,512]{1,0:T(8,128)S(1)} copy-done((f32[192,512]{1,0:T(8,128)S(1)}, f32[192,512]{1,0:T(8,128)}, u32[]{:S(2)}) %copy-start) | copy-done | bytes 393240
  2.4 0.0 copy-start.1
  2.4 0.7 %copy-done.1 = f32[192]{0:T(256)S(1)} copy-done((f32[192]{0:T(256)S(1)}, f32[192]{0:T(256)}, u32[]{:S(2)}) %copy-start.1) | copy-done | bytes 792
  3.1 0.0 copy-start.2
  3.1 0.7 %copy-done.2 = s32[8]{0:T(128)S(1)} copy-done((s32[8]{0:T(128)S(1)}, s32[8]{0:T(128)}, u32[]{:S(2)}) %copy-start.2) | copy-done | bytes 56
  3.7 0.0 copy-start.3
  3.7 0.7 %copy-done.3 = s32[8]{0:T(128)S(1)} copy-done((s32[8]{0:T(128)S(1)}, s32[8]{0:T(128)}, u32[]{:S(2)}) %copy-start.3) | copy-done | bytes 56
  4.4 53.6 %shard_map.77 = (f32[8,192,512]{2,1,0:T(8,128)S(1)}, f32[4,128]{1,0:T(4,128)S(1)}) custom-call(s32[8]{0:T(128)S(1)} %copy-done.2, s32[8]{0:T(128)S(1)} %copy-done.3, f32[32,4]{1,0:T(8,128)S(1)} %copy.8.table_hbm, f32[1,192]{1,0:T(1,128)S(1)} %bitcast.3, f32[8,192,512]{2,1,0:T(8,128)} %m_hbm.1, f32[192,512]{1,0:T(8,128)S(1)} %copy-done), custom_call_target="tpu_custom_call" | custom-call | tf_op jit(solution)/shard_map/pallas_call | solution.py:482
  57.9 1.7 %copy.11 = f32[8,192,512]{2,1,0:T(8,128)} copy(f32[8,192,512]{2,1,0:T(8,128)S(1)} %get-tuple-element.8) | data formatting | bytes 6291456
  59.6 0.6 copy.12
Async XLA Ops:
  1.4 1.0 %copy-start = (f32[192,512]{1,0:T(8,128)S(1)}, f32[192,512]{1,0:T(8,128)}, u32[]{:S(2)}) copy-start(f32[192,512]{1,0:T(8,128)} %x0_hbm.1) | copy-start | bytes 1179652
  2.4 0.7 %copy-start.1 = (f32[192]{0:T(256)S(1)}, f32[192]{0:T(256)}, u32[]{:S(2)}) copy-start(f32[192]{0:T(256)} %param.10) | copy-start | bytes 2308
  3.1 0.7 %copy-start.2 = (s32[8]{0:T(128)S(1)}, s32[8]{0:T(128)}, u32[]{:S(2)}) copy-start(s32[8]{0:T(128)} %seg_hbm.1) | copy-start | bytes 100
  3.7 0.7 %copy-start.3 = (s32[8]{0:T(128)S(1)}, s32[8]{0:T(128)}, u32[]{:S(2)}) copy-start(s32[8]{0:T(128)} %obs_hbm.1) | copy-start | bytes 100

commit v4 on v3

--- a/solution.py
+++ b/solution.py
@@ -165,8 +165,13 @@
         keep[0, pl.ds(v * 8, 8), :] = jnp.ones((8, 128), F32)
         keep[1, pl.ds(v * 8, 8), :] = 1.0 - g
 
+    seg_row = lax.broadcasted_iota(jnp.int32, (8, SEGS), 0)
+    seg_lane = lax.broadcasted_iota(jnp.int32, (8, SEGS), 1)
     for c in range(CABLES):
-        tab[c] = jnp.broadcast_to(table_ref[:, c : c + 1], (SEGS, 128))
+        for s in range(SEGS // 8):
+            g = jnp.broadcast_to(table_ref[c : c + 1, :], (8, SEGS))
+            g = jnp.where(seg_lane == seg_row + s * 8, g, F32(0.0))
+            tab[c, s * 8 : s * 8 + 8, :] = jnp.broadcast_to(jnp.sum(g, axis=1, keepdims=True), (8, 128))
 
     def spread_w(s):
         return [jnp.broadcast_to(tab[c, pl.ds(s, 1), :], (8, 128)) for c in range(CABLES)]
@@ -464,7 +469,9 @@
             power = power + powers[slot + k]
         slot += count
     total_steps = here * ring * nx * nz
-    power_ref[...] = power[0:tiles] / F32(total_steps * STATES)
+    power = power / F32(total_steps * STATES)
+    for f in range(tiles):
+        power_ref[0:1, f * 128 : f * 128 + 128] = power[f : f + 1]
     for c in stores:
         c.wait()
 
@@ -476,21 +483,21 @@
     tiles = runs // 128
     gains = filter_gains.reshape(1, STATES)
     vmem = pl.BlockSpec(memory_space=pltpu.VMEM)
-    hbm = pl.BlockSpec(memory_space=pl.ANY)
+    hbm = pl.BlockSpec(memory_space=pltpu.HBM)
     dma = pltpu.SemaphoreType.DMA
     packed = (SIDE, 128)
     filtered, power = pl.pallas_call(
         functools.partial(kernel, dims, runs, here),
         out_shape=(
             jax.ShapeDtypeStruct(measurements.shape, F32),
-            jax.ShapeDtypeStruct((tiles, 128), F32),
+            jax.ShapeDtypeStruct((1, runs), F32),
         ),
         in_specs=[hbm] * 6,
         out_specs=(hbm, vmem),
         scratch_shapes=[
             pltpu.SMEM((here,), jnp.int32),
             pltpu.SMEM((here,), jnp.int32),
-            pltpu.VMEM((SEGS, CABLES), F32),
+            pltpu.VMEM((CABLES, SEGS), F32),
             pltpu.VMEM((1, STATES), F32),
             dma((4,)),
             pltpu.VMEM((tiles, here, STATES, 128), F32),
@@ -543,7 +550,7 @@
         compiler_params=pltpu.CompilerParams(
             collective_id=0, has_side_effects=True, vmem_limit_bytes=48 << 20
         ),
-    )(segment_ids, observed, courant_table, gains, measurements, initial_state)
+    )(segment_ids, observed, courant_table.T, gains, measurements, initial_state)
     return filtered, power.reshape(runs)
 
 

time: 60.4 us -> 60.3 us (level)
    unnamed x11 -> x12, local copies, waits for them, and re-layouts: 5.99 us -> 5.9 us
where the time goes in v4:
time: 60.3 us; the launch traced here: 60.1 us
  Pallas kernels  53.5 us (89%)
  local copies, waits for them, and re-layouts  5.9 us (10%)
  between operations  0.65 us (1%)
    pallas_call x1, Pallas kernels, local(): pl.pallas_call(functools.partial(kernel, dims, runs, here), out_shape=(ja...  53.5 us
    unnamed x12, local copies, waits for them, and re-layouts  5.9 us

profile of v4, /device:TPU:0, one launch (start us, length us, event | category | flops | bytes accessed | tf_op | source)
XLA Modules:
  0.0 60.1 jit_solution(14556289726858624523)
XLA Ops:
  0.6 0.0 copy-start
  0.6 1.0 %copy-done = f32[192,512]{1,0:T(8,128)S(1)} copy-done((f32[192,512]{1,0:T(8,128)S(1)}, f32[192,512]{1,0:T(8,128)}, u32[]{:S(2)}) %copy-start) | copy-done | bytes 393240
  1.6 0.0 copy-start.1
  1.6 0.7 %copy-done.1 = f32[32,4]{0,1:T(4,128)S(1)} copy-done((f32[32,4]{0,1:T(4,128)S(1)}, f32[32,4]{0,1:T(4,128)}, u32[]{:S(2)}) %copy-start.1) | copy-done | bytes 536
  2.3 0.0 copy-start.2
  2.3 0.7 %copy-done.2 = f32[192]{0:T(256)S(1)} copy-done((f32[192]{0:T(256)S(1)}, f32[192]{0:T(256)}, u32[]{:S(2)}) %copy-start.2) | copy-done | bytes 792
  3.0 0.0 copy-start.3
  3.0 0.7 %copy-done.3 = s32[8]{0:T(128)S(1)} copy-done((s32[8]{0:T(128)S(1)}, s32[8]{0:T(128)}, u32[]{:S(2)}) %copy-start.3) | copy-done | bytes 56
  3.6 0.0 copy-start.4
  3.6 0.7 %copy-done.4 = s32[8]{0:T(128)S(1)} copy-done((s32[8]{0:T(128)S(1)}, s32[8]{0:T(128)}, u32[]{:S(2)}) %copy-start.4) | copy-done | bytes 56
  4.3 53.5 %shard_map.77 = (f32[8,192,512]{2,1,0:T(8,128)S(1)}, f32[1,512]{1,0:T(1,128)S(1)}) custom-call(s32[8]{0:T(128)S(1)} %copy-done.3, s32[8]{0:T(128)S(1)} %copy-done.4, f32[4,32]{1,0:T(4,128)S(1)} %bitcast.3, f32[1,192]{1,0:T(1,128)S(1)} %bitcast.5, f32[8,192,512]{2,1,0:T(8,128)} %m_hbm.1, f32[192,512]{1,0:T(8,128)S(1)} %copy-done), custom_call_target="tpu_custom_call" | custom-call | tf_op jit(solution)/shard_map/pallas_call | solution.py:489
  57.8 1.7 %copy.10 = f32[8,192,512]{2,1,0:T(8,128)} copy(f32[8,192,512]{2,1,0:T(8,128)S(1)} %get-tuple-element.8) | data formatting | bytes 6291456
  59.5 0.6 copy.11
Async XLA Ops:
  0.6 1.0 %copy-start = (f32[192,512]{1,0:T(8,128)S(1)}, f32[192,512]{1,0:T(8,128)}, u32[]{:S(2)}) copy-start(f32[192,512]{1,0:T(8,128)} %x0_hbm.1) | copy-start | bytes 1179652
  1.6 0.7 %copy-start.1 = (f32[32,4]{0,1:T(4,128)S(1)}, f32[32,4]{0,1:T(4,128)}, u32[]{:S(2)}) copy-start(f32[32,4]{0,1:T(4,128)} %param.9) | copy-start | bytes 1540
  2.3 0.7 %copy-start.2 = (f32[192]{0:T(256)S(1)}, f32[192]{0:T(256)}, u32[]{:S(2)}) copy-start(f32[192]{0:T(256)} %param.10) | copy-start | bytes 2308
  3.0 0.7 %copy-start.3 = (s32[8]{0:T(128)S(1)}, s32[8]{0:T(128)}, u32[]{:S(2)}) copy-start(s32[8]{0:T(128)} %seg_hbm.1) | copy-start | bytes 100
  3.6 0.7 %copy-start.4 = (s32[8]{0:T(128)S(1)}, s32[8]{0:T(128)}, u32[]{:S(2)}) copy-start(s32[8]{0:T(128)} %obs_hbm.1) | copy-start | bytes 100
